TPU v7x, 128 devices: a whole 4x4x4 slice. The times are simulated.
128 devices in a mesh: blk: 8 (over z_lo, x), head: 16 (over y, z_hi, core).
Axes of the slice: x: 4, y: 4, z: 4 (z_hi: 2, z_lo: 2; z = z_hi * 2 + z_lo), core: 2. Of those that a mesh axis runs over, the one named last changes fastest.
Arguments:
- qkv: bfloat16 [32768, 6144], P(('blk', 'head')), may hold values from -12 to 12
Outputs:
- attended: bfloat16 [32768, 2048], P(('blk', 'head'))
All inputs are finite; a program needn't handle non-finite values.
Results may differ from a plain program's by a relative error of at most 0.0059.
Values may be sent and summed in bfloat16 or wider, within the bound.
A program may use at most 128 MiB of HBM per device.

v0:
```python
import jax
import jax.numpy as jnp
from jax import lax
from jax.sharding import PartitionSpec as P

HEAD_DIM = 64
BLOCK = 2048
BLK_DEV = 2


def attend(query, pair):
    keys = pair[:, 0]
    values = pair[:, 1]
    tile = min(512, BLOCK)
    scale = HEAD_DIM ** (-0.5)

    def one_tile(query_tile):
        scores = (
            jnp.einsum("qhd,khd->hqk", query_tile, keys, preferred_element_type=jnp.float32) * scale
        )
        row_max = jnp.max(scores, axis=-1)
        probs = jnp.exp(scores - row_max[..., None]).astype(jnp.bfloat16)
        total = jnp.sum(probs.astype(jnp.float32), axis=-1)
        weighted = jnp.einsum("hqk,khd->hqd", probs, values, preferred_element_type=jnp.float32)
        return (row_max, total, weighted)

    tiles = query.reshape(BLOCK // tile, tile, query.shape[1], query.shape[2])
    return lax.map(one_tile, tiles)


def combine(partials):
    overall = partials[0][0]
    for entry in partials[1:]:
        overall = jnp.maximum(overall, entry[0])
    numer = jnp.zeros_like(partials[0][2])
    denom = jnp.zeros_like(partials[0][1])
    for row_max, total, weighted in partials:
        factor = jnp.exp(row_max - overall)
        numer = numer + factor[..., None] * weighted
        denom = denom + factor * total
    result = numer / denom[..., None]
    return result.transpose(0, 2, 1, 3).reshape(BLOCK, result.shape[1] * result.shape[3])


def on_device(qkv):
    rows = qkv.shape[0]
    heads_cols = qkv.shape[1] // 3
    shaped = qkv.reshape(rows, 3, heads_cols)
    grouped = lax.all_to_all(shaped, "head", split_axis=2, concat_axis=0, tiled=True)
    local_cols = grouped.shape[2]
    heads_here = local_cols // HEAD_DIM
    grid = grouped.reshape(BLK_DEV, BLOCK, 3, heads_here, HEAD_DIM)
    queries = grid[:, :, 0]
    pairs = grid[:, :, 1:3]
    device_bits = lax.axis_size("blk").bit_length() - 1
    partials = [[] for j in range(BLK_DEV)]

    def own_blocks():
        for j in range(BLK_DEV):
            partials[j].append(attend(queries[j], pairs[j]))
            partials[j].append(attend(queries[j], pairs[j ^ 1 << 0]))

    gathered = lax.all_gather(pairs, "blk", axis=0, tiled=True)
    mine = lax.axis_index("blk")
    for bit in range(device_bits):
        for j in range(BLK_DEV):
            where = jnp.bitwise_xor(mine, 1 << bit) * BLK_DEV + j
            chosen = lax.dynamic_index_in_dim(gathered, where, 0, keepdims=False)
            partials[j].append(attend(queries[j], chosen))
    own_blocks()
    outputs = jnp.concatenate([combine(partials[j]) for j in range(BLK_DEV)], axis=0).astype(
        jnp.bfloat16
    )
    return lax.all_to_all(outputs, "head", split_axis=0, concat_axis=1, tiled=True)


def solution(mesh):
    in_specs = (P(("blk", "head"), None),)
    out_specs = P(("blk", "head"), None)
    return jax.shard_map(
        on_device, mesh=mesh, in_specs=in_specs, out_specs=out_specs, check_vma=False
    )
```

profile of v0, /device:TPU:1, one launch (start us, length us, event | category | flops | bytes accessed | tf_op | source)
XLA Modules:
  0.0 471.4 jit_solution(7720879860149030022)
XLA Ops:
  6.5 3.2 copy.39
  9.7 17.2 %copy.40 = bf16[256,3,2048]{0,1,2:T(4,128)(2,1)} copy(bf16[256,3,2048]{0,2,1:T(8,128)(2,1)S(1)} %bitcast.366) | data formatting | bytes 6291456 | tf_op jit(solution)/shard_map/reshape | solution.py:48
  26.9 9.3 %all-to-all-start = ((bf16[256,3,2048]{0,1,2:T(4,128)(2,1)}), bf16[256,3,2048]{0,1,2:T(4,128)(2,1)}, u32[]{:S(2)}, u32[]{:S(2)}) async-start(bf16[256,3,2048]{0,1,2:T(4,128)(2,1)} %copy.40), calls=%async_computation | async-start | bytes 8388608 | tf_op jit(solution)/shard_map/all_to_all | solution.py:49
  36.2 52.6 %all-to-all-done = bf16[256,3,2048]{0,1,2:T(4,128)(2,1)} async-done(((bf16[256,3,2048]{0,1,2:T(4,128)(2,1)}), bf16[256,3,2048]{0,1,2:T(4,128)(2,1)}, u32[]{:S(2)}, u32[]{:S(2)}) %all-to-all-start) | async-done | bytes 3145760 | tf_op jit(solution)/shard_map/all_to_all | solution.py:49
  88.9 2.6 copy.41
  91.5 3.5 copy.42
  95.0 4.2 reshape.47
  101.1 5.2 %slice_reduce_fusion.1 = (bf16[2048,2,64]{0,2,1:T(8,128)(2,1)}, bf16[2048,2,64]{0,2,1:T(8,128)(2,1)}) fusion(bf16[2,2048,3,2,64]{1,0,4,3,2:T(2,128)(2,1)S(1)} %reshape.47), kind=kLoop, calls=%fused_computation.121 | loop fusion | bytes 2097152 | tf_op jit(solution)/shard_map/slice | solution.py:69
  106.3 4.2 fusion.62
  115.0 2.9 copy_bitcast_fusion
  119.2 21.6 %while.143 = (s32[]{:T(128)}, f32[4,2,512]{2,1,0:T(2,128)S(1)}, f32[4,2,512]{2,1,0:T(2,128)S(1)}, f32[4,2,512,64]{2,3,1,0:T(8,128)}, bf16[4,512,2,64]{1,3,2,0:T(...) while((s32[]{:T(128)}, f32[4,2,512]{2,1,0:T(2,128)S(1)}, ...), condition=%wide.region_15.16_spmd, body=%wide.region_12.15_spmd.sunk | while | flops 557840384 | bytes 26640988 | solution.py:28
  122.2 2.4 fusion.124
  127.6 2.3 fusion.124
  133.0 2.4 fusion.124
  138.4 2.4 fusion.124
  142.0 21.8 %while.144 = (s32[]{:T(128)}, f32[4,2,512]{2,1,0:T(2,128)S(1)}, f32[4,2,512]{2,1,0:T(2,128)S(1)}, f32[4,2,512,64]{2,3,1,0:T(8,128)}, bf16[4,512,2,64]{1,3,2,0:T(...) while((s32[]{:T(128)}, f32[4,2,512]{2,1,0:T(2,128)S(1)}, ...), condition=%wide.region_19.20_spmd, body=%wide.region_16.19_spmd.sunk | while | flops 557840384 | bytes 26640988 | solution.py:28
  145.2 2.4 fusion.127
  150.6 2.4 fusion.127
  156.0 2.4 fusion.127
  161.5 2.4 fusion.127
  165.0 21.6 %while.148 = (s32[]{:T(128)}, f32[4,2,512]{2,1,0:T(2,128)S(1)}, f32[4,2,512]{2,1,0:T(2,128)S(1)}, f32[4,2,512,64]{2,3,1,0:T(8,128)}, bf16[4,512,2,64]{1,3,2,0:T(...) while((s32[]{:T(128)}, f32[4,2,512]{2,1,0:T(2,128)S(1)}, ...), condition=%wide.region_35.36_spmd, body=%wide.region_32.35_spmd.sunk | while | flops 557840384 | bytes 26640988 | solution.py:28
  168.0 2.3 fusion.139
  173.4 2.4 fusion.139
  178.8 2.4 fusion.139
  184.2 2.4 fusion.139
  187.2 19.9 %while.149 = (s32[]{:T(128)}, f32[4,2,512]{2,1,0:T(2,128)S(1)}, f32[4,2,512]{2,1,0:T(2,128)S(1)}, f32[4,2,512,64]{2,3,1,0:T(8,128)S(1)}, bf16[4,512,2,64]{1,3,2,...) while((s32[]{:T(128)}, f32[4,2,512]{2,1,0:T(2,128)S(1)}, ...), condition=%wide.region_39.40_spmd, body=%wide.region_36.39_spmd.sunk | while | flops 557840384 | bytes 26640480 | solution.py:28
  207.1 83.3 %all-gather.2.cloned.1.call-done = bf16[16,2048,2,2,64]{1,4,3,2,0:T(8,128)(2,1)} async-done(((bf16[2,2048,2,2,64]{1,4,3,2,0:T(8,128)(2,1)}), bf16[16,2048,2,2,64]{1,4,3,2,0:T(8,128)(2,1)}) %all-gather.2.cloned.1.call-update) | async-done | bytes 16777232 | tf_op jit(solution)/shard_map/all_gather | solution.py:63
  290.4 5.3 %dynamic-slice_bitcast_fusion.5 = (bf16[2048,2,2,64]{0,3,2,1:T(8,128)(2,1)S(1)}, bf16[2048,2,2,64]{0,3,2,1:T(8,128)(2,1)}, bf16[2048,2,2,64]{0,3,2,1:T(8,128)(2,...) fusion(bf16[16,2048,2,2,64]{1,4,3,2,0:T(8,128)(2,1)} %all-gather.2., ...), kind=kLoop, calls=%fused_computation.132 | loop fusion | bytes 12582936 | tf_op jit(solution)/shard_map/jit(dynamic_index_in_dim)/squeeze | solution.py:68
  297.2 21.8 %while.140 = (s32[]{:T(128)}, f32[4,2,512]{2,1,0:T(2,128)S(1)}, f32[4,2,512]{2,1,0:T(2,128)S(1)}, f32[4,2,512,64]{2,3,1,0:T(8,128)}, bf16[4,512,2,64]{1,3,2,0:T(...) while((s32[]{:T(128)}, f32[4,2,512]{2,1,0:T(2,128)S(1)}, ...), condition=%wide.region_3.4_spmd, body=%wide.region_0.3_spmd.sunk | while | flops 557840384 | bytes 26640988 | solution.py:28
  300.4 2.4 fusion.115
  305.8 2.4 fusion.115
  311.2 2.4 fusion.115
  316.6 2.4 fusion.115
  319.1 19.9 %while.141 = (s32[]{:T(128)}, f32[4,2,512]{2,1,0:T(2,128)S(1)}, f32[4,2,512]{2,1,0:T(2,128)S(1)}, f32[4,2,512,64]{2,3,1,0:T(8,128)S(1)}, bf16[4,512,2,64]{1,3,2,...) while((s32[]{:T(128)}, f32[4,2,512]{2,1,0:T(2,128)S(1)}, ...), condition=%wide.region_7.8_spmd, body=%wide.region_4.7_spmd.sunk | while | flops 557840384 | bytes 26640480 | solution.py:28
  342.9 21.6 %while.142 = (s32[]{:T(128)}, f32[4,2,512]{2,1,0:T(2,128)S(1)}, f32[4,2,512]{2,1,0:T(2,128)S(1)}, f32[4,2,512,64]{2,3,1,0:T(8,128)}, bf16[4,512,2,64]{1,3,2,0:T(...) while((s32[]{:T(128)}, f32[4,2,512]{2,1,0:T(2,128)S(1)}, ...), condition=%wide.region_11.12_spmd, body=%wide.region_8.11_spmd.sunk | while | flops 557840384 | bytes 26640988 | solution.py:28
  345.9 2.4 fusion.121
  351.3 2.4 fusion.121
  362.1 2.4 fusion.121
  364.5 3.2 fusion.60
  368.4 20.1 %while.145 = (s32[]{:T(128)}, f32[4,2,512]{2,1,0:T(2,128)S(1)}, f32[4,2,512]{2,1,0:T(2,128)S(1)}, f32[4,2,512,64]{2,3,1,0:T(8,128)S(1)}, bf16[4,512,2,64]{1,3,2,...) while((s32[]{:T(128)}, f32[4,2,512]{2,1,0:T(2,128)S(1)}, ...), condition=%wide.region_23.24_spmd, body=%wide.region_20.23_spmd.sunk | while | flops 557840384 | bytes 26640480 | solution.py:28
  392.4 21.6 %while.146 = (s32[]{:T(128)}, f32[4,2,512]{2,1,0:T(2,128)S(1)}, f32[4,2,512]{2,1,0:T(2,128)S(1)}, f32[4,2,512,64]{2,3,1,0:T(8,128)}, bf16[4,512,2,64]{1,3,2,0:T(...) while((s32[]{:T(128)}, f32[4,2,512]{2,1,0:T(2,128)S(1)}, ...), condition=%wide.region_27.28_spmd, body=%wide.region_24.27_spmd.sunk | while | flops 557840384 | bytes 26640988 | solution.py:28
  395.4 2.4 fusion.133
  400.8 2.4 fusion.133
  406.3 2.4 fusion.133
  411.7 2.4 fusion.133
  414.2 19.9 %while.147 = (s32[]{:T(128)}, f32[4,2,512]{2,1,0:T(2,128)S(1)}, f32[4,2,512]{2,1,0:T(2,128)S(1)}, f32[4,2,512,64]{2,3,1,0:T(8,128)S(1)}, bf16[4,512,2,64]{1,3,2,...) while((s32[]{:T(128)}, f32[4,2,512]{2,1,0:T(2,128)S(1)}, ...), condition=%wide.region_31.32_spmd, body=%wide.region_28.31_spmd.sunk | while | flops 557840384 | bytes 26640480 | solution.py:28
  434.2 2.9 fusion.61
  438.4 23.8 %all_to_all.31 = bf16[16,256,128]{2,1,0:T(8,128)(2,1)S(1)} all-to-all(bf16[16,256,128]{2,1,0:T(8,128)(2,1)S(1)} %bitcast.367), channel_id=1, replica_groups=mesh['blk'=8,'head'=16] {'head'}, dimensions={0} | all-to-all | bytes 2097152 | tf_op jit(solution)/shard_map/all_to_all | solution.py:74
  (228 shorter events, 178.0 us)
Async XLA Ops:
  26.9 62.0 %all-to-all-start = ((bf16[256,3,2048]{0,1,2:T(4,128)(2,1)}), bf16[256,3,2048]{0,1,2:T(4,128)(2,1)}, u32[]{:S(2)}, u32[]{:S(2)}) async-start(bf16[256,3,2048]{0,1,2:T(4,128)(2,1)} %copy.40), calls=%async_computation | async-start | bytes 8388608 | tf_op jit(solution)/shard_map/all_to_all | solution.py:49
  36.2 254.2 %all-gather.2.cloned.1.call-start = ((), (), s32[]{:S(2)}) async-start(), calls=%async_computation.2 | async-start | bytes 18874368 | tf_op jit(solution)/shard_map/all_gather | solution.py:63
  110.5 4.5 copy-start
  140.8 1.2 copy-start.4
  140.8 1.2 copy-start.6
  163.8 1.1 copy-start.8
  163.8 1.1 copy-start.10
  186.6 0.6 copy-start.12
  186.6 0.6 copy-start.14
  207.1 88.7 %copy-start.1 = (f32[4,2,512,64]{2,3,1,0:T(8,128)}, f32[4,2,512,64]{2,3,1,0:T(8,128)S(1)}, u32[]{:S(2)}) copy-start(f32[4,2,512,64]{2,3,1,0:T(8,128)S(1)} %get-tuple-element.419) | copy-start | bytes 3145732
  207.1 88.9 %copy-start.16 = (f32[4,2,512]{2,1,0:T(2,128)}, f32[4,2,512]{2,1,0:T(2,128)S(1)}, u32[]{:S(2)}) copy-start(f32[4,2,512]{2,1,0:T(2,128)S(1)} %get-tuple-element.414) | copy-start | bytes 49156
  207.1 88.9 %copy-start.18 = (f32[4,2,512]{2,1,0:T(2,128)}, f32[4,2,512]{2,1,0:T(2,128)S(1)}, u32[]{:S(2)}) copy-start(f32[4,2,512]{2,1,0:T(2,128)S(1)} %get-tuple-element.424) | copy-start | bytes 49156
  339.1 1.0 copy-start.2
  342.8 21.6 %copy-start.5 = (f32[4,2,512]{2,1,0:T(2,128)S(1)}, f32[4,2,512]{2,1,0:T(2,128)}, u32[]{:S(2)}) copy-start(f32[4,2,512]{2,1,0:T(2,128)} %copy-done.4) | copy-start | bytes 49156
  342.8 21.6 %copy-start.7 = (f32[4,2,512]{2,1,0:T(2,128)S(1)}, f32[4,2,512]{2,1,0:T(2,128)}, u32[]{:S(2)}) copy-start(f32[4,2,512]{2,1,0:T(2,128)} %copy-done.6) | copy-start | bytes 49156
  342.8 21.6 %copy-start.9 = (f32[4,2,512]{2,1,0:T(2,128)S(1)}, f32[4,2,512]{2,1,0:T(2,128)}, u32[]{:S(2)}) copy-start(f32[4,2,512]{2,1,0:T(2,128)} %copy-done.8) | copy-start | bytes 49156
  342.9 21.6 %copy-start.11 = (f32[4,2,512]{2,1,0:T(2,128)S(1)}, f32[4,2,512]{2,1,0:T(2,128)}, u32[]{:S(2)}) copy-start(f32[4,2,512]{2,1,0:T(2,128)} %copy-done.10) | copy-start | bytes 49156
  388.6 1.0 copy-start.3
  414.2 20.0 %copy-start.13 = (f32[4,2,512]{2,1,0:T(2,128)S(1)}, f32[4,2,512]{2,1,0:T(2,128)}, u32[]{:S(2)}) copy-start(f32[4,2,512]{2,1,0:T(2,128)} %copy-done.12) | copy-start | bytes 49156
  414.2 20.0 %copy-start.15 = (f32[4,2,512]{2,1,0:T(2,128)S(1)}, f32[4,2,512]{2,1,0:T(2,128)}, u32[]{:S(2)}) copy-start(f32[4,2,512]{2,1,0:T(2,128)} %copy-done.14) | copy-start | bytes 49156
  414.2 20.0 %copy-start.17 = (f32[4,2,512]{2,1,0:T(2,128)S(1)}, f32[4,2,512]{2,1,0:T(2,128)}, u32[]{:S(2)}) copy-start(f32[4,2,512]{2,1,0:T(2,128)} %copy-done.16) | copy-start | bytes 49156
  414.2 20.0 %copy-start.19 = (f32[4,2,512]{2,1,0:T(2,128)S(1)}, f32[4,2,512]{2,1,0:T(2,128)}, u32[]{:S(2)}) copy-start(f32[4,2,512]{2,1,0:T(2,128)} %copy-done.18) | copy-start | bytes 49156
Sparse Core Ops, SparseCore 0:
  112.9 177.4 all-gather.1
where the time goes:
time: 477 us; the launch traced here: 471 us
  matrix products  142 us (30%)
  waiting for transfers between devices  136 us (29%)
  local copies, waits for them, and re-layouts  72.3 us (15%)
  other arithmetic  71.9 us (15%)
  blocking collectives  23.8 us (5%)
  between operations  14.4 us (3%)
  starting transfers between devices  9.34 us (2%)
    dot_general x40, matrix products, one_tile(): jnp.einsum('hqk,khd->hqd', probs, values, preferred_element_type=jnp.floa...  87 us
    all_gather x1, waiting for transfers between devices, on_device(): gathered = lax.all_gather(pairs, 'blk', axis=0, tiled=True)  83.3 us
    reduce_sum x40, other arithmetic, one_tile(): total = jnp.sum(probs.astype(jnp.float32), axis=-1)  65.6 us
    dot_general x40, matrix products, one_tile(): jnp.einsum('qhd,khd->hqk', query_tile, keys, preferred_element_type=jnp.f...  55.4 us
    all_to_all x1, waiting for transfers between devices, on_device(): lax.all_to_all(shaped, 'head', split_axis=2, concat_axis=0, tiled=True)  52.6 us
    all_to_all x1, blocking collectives, on_device(): lax.all_to_all(outputs, 'head', split_axis=0, concat_axis=1, tiled=True)  23.8 us
    reshape x1, local copies, waits for them, and re-layouts, on_device(): shaped = qkv.reshape(rows, 3, heads_cols)  17.2 us
  transfers between devices with their start and end apart: 2, of which 2 were waited for; matrix products, arithmetic and copies ran while one was open for 20% of the time, Pallas kernels for 0%

commit v1 on v0

v1 whole, which is shorter than its diff:
```python
import math

import jax
import jax.numpy as jnp
from jax import lax
from jax.experimental import pallas as pl
from jax.experimental.pallas import tpu as pltpu
from jax.sharding import PartitionSpec as P

HEAD_DIM = 64
BLOCK = 2048
NBLK = 16
HEADS = 32
D = HEADS * HEAD_DIM
CHIPS = 64
ROWS = 256
PART = 64
QT = 512
KC = 512
PAIRS = 5 * NBLK
SCALE = HEAD_DIM ** -0.5 * math.log2(math.e)
MESH_ID = pl.DeviceIdType.MESH


def xor(a, b, bits):
    total = 0
    for i in range(bits):
        w = 1 << i
        total = total + w * lax.rem(lax.rem(lax.div(a, w), 2) + lax.rem(lax.div(b, w), 2), 2)
    return total


def pair_of(n):
    c = lax.div(n, 5)
    i = lax.rem(n, 5)
    w = jnp.where(i == 4, 0, jnp.where(i == 0, 1, jnp.where(i == 1, 2, jnp.where(i == 2, 4, 8))))
    return xor(c, w, 4), c


def kernel(
    x_ref, out_ref,
    sendq, sendkv, qb, kvb, qs, kk, va, m_ref, acc, s0, s1, al0, al1, mn0, mn1, osend, obuf,
    q_send, q_recv, kv_send, kv_recv, f_send, f_recv, o_send, o_recv, loc,
):
    blk = lax.axis_index("blk")
    head = lax.axis_index("head")
    chip = blk * 8 + lax.div(head, 2)
    core = lax.rem(head, 2)
    f32, bf16 = jnp.float32, jnp.bfloat16

    def dev(c):
        return (lax.div(c, 8), lax.rem(c, 8) * 2 + core)

    sibling = (blk, head + 1 - 2 * core)

    barrier = pltpu.get_barrier_semaphore()

    @pl.loop(1, CHIPS)
    def _(t):
        pl.semaphore_signal(barrier, inc=1, device_id=dev(xor(chip, t, 6)), device_id_type=MESH_ID)

    pl.semaphore_signal(barrier, inc=1, device_id=sibling, device_id_type=MESH_ID)

    @pl.loop(0, HEADS // 2)
    def _(g):
        x = x_ref[:, pl.ds(pl.multiple_of(g * 128, 128), 128)]
        for e in range(2):
            y = x[:, e * 64:(e + 1) * 64]
            for c in range(2):
                sendq[g * 4 + e * 2 + c] = jnp.concatenate(
                    [y[c * 128:c * 128 + 64], y[c * 128 + 64:c * 128 + 128]], axis=1
                )

    pl.semaphore_wait(barrier, CHIPS)

    @pl.loop(1, CHIPS)
    def _(t):
        to = xor(chip, t, 6)
        pltpu.make_async_remote_copy(
            sendq.at[to], qb.at[t], q_send, q_recv, device_id=dev(to), device_id_type=MESH_ID
        ).start()

    @pl.loop(0, HEADS // 2)
    def _(g):
        k = x_ref[:, pl.ds(pl.multiple_of(D + g * 128, 128), 128)]
        v = x_ref[:, pl.ds(pl.multiple_of(2 * D + g * 128, 128), 128)]
        for e in range(2):
            h = slice(e * 64, (e + 1) * 64)
            sendkv[g * 2 + e] = jnp.concatenate([k[:, h], v[:, h]], axis=1)

    @pl.loop(1, CHIPS)
    def _(t):
        to = xor(chip, t, 6)
        pltpu.make_async_remote_copy(
            sendkv.at[lax.div(to, 2)], kvb.at[core, t], kv_send, kv_recv.at[lax.div(t, 4)],
            device_id=dev(to), device_id_type=MESH_ID,
        ).start()

    own_q = pltpu.make_async_copy(sendq.at[chip], qb.at[0], loc.at[0])
    own_kv = pltpu.make_async_copy(sendkv.at[lax.div(chip, 2)], kvb.at[core, 0], loc.at[1])
    own_q.start()
    own_kv.start()

    def forward(c):
        rows = pl.ds(c * 4, 4)
        return pltpu.make_async_remote_copy(
            kvb.at[core, rows], kvb.at[core, rows], f_send, f_recv.at[c],
            device_id=sibling, device_id_type=MESH_ID,
        )

    def landed(c, skip):
        part = kvb.at[core, pl.ds(c * 4 + skip, 4 - skip)]
        pltpu.make_async_remote_copy(
            part, part, kv_send, kv_recv.at[c], device_id=sibling, device_id_type=MESH_ID
        ).wait_recv()

    def arrive(c):
        landed(c, 0)
        forward(c).start()

    def ready(c):
        part = kvb.at[1 - core, pl.ds(c * 4, 4)]
        pltpu.make_async_remote_copy(
            part, part, f_send, f_recv.at[c], device_id=sibling, device_id_type=MESH_ID
        ).wait_recv()
        slot = lax.rem(c, 2)
        low = lax.broadcasted_iota(jnp.int32, (ROWS, 128), 1) < 64

        @pl.loop(0, 2)
        def _(z):
            @pl.loop(0, 4)
            def _(w):
                t = kvb[z, c * 4 + w]
                rows = pl.ds(pl.multiple_of((z * 4 + w) * ROWS, ROWS), ROWS)
                kk[slot, rows] = jnp.concatenate([t[:, :64], t[:, :64]], axis=1)
                va[slot, rows] = jnp.where(low, jnp.ones_like(t), t)

    own_kv.wait()
    landed(0, 1)
    forward(0).start()

    m_ref[...] = jnp.full_like(m_ref, -jnp.inf)
    acc[...] = jnp.zeros_like(acc)

    own_q.wait()
    qall = qb.at[pl.ds(1, CHIPS - 1)]
    pltpu.make_async_remote_copy(
        qall, qall, q_send, q_recv, device_id=sibling, device_id_type=MESH_ID
    ).wait_recv()

    @pl.loop(0, NBLK)
    def _(a):
        x = qb[pl.ds(a * 4, 4)].reshape(ROWS, 128).astype(f32) * SCALE
        hi = x.astype(bf16)
        lo = (x - hi.astype(f32)).astype(bf16)
        qs[a, 0:ROWS] = jnp.concatenate([hi[:, :64], lo[:, :64]], axis=1)
        qs[a, ROWS:QT] = jnp.concatenate([hi[:, 64:], lo[:, 64:]], axis=1)

    def stage(na, nb, sa, sb, ala, alb, mna, mnb):
        if na is not None:
            a, c = pair_of(na)
            kslot = lax.rem(c, 2)
            q = qs[a]
            m_old = m_ref[a]
            mx = None
        if nb is not None:
            a2, c2 = pair_of(nb)
            vslot = lax.rem(c2, 2)
            m_b = mnb[...]
            o = None
        for j in range(BLOCK // KC):
            ks = slice(j * KC, (j + 1) * KC)
            if na is not None:
                s = lax.dot_general(
                    q, kk[kslot, ks], (((1,), (1,)), ((), ())), preferred_element_type=f32
                )
                sa[:, ks] = s
                for l in range(KC // 128):
                    t = s[:, l * 128:(l + 1) * 128]
                    mx = t if mx is None else jnp.maximum(mx, t)
            if nb is not None:
                ps = []
                for l in range(KC // 128):
                    at = j * KC + l * 128
                    ps.append(jnp.exp2(sb[:, at:at + 128] - m_b).astype(bf16))
                p = jnp.concatenate(ps, axis=1)
                part = jnp.dot(p, va[vslot, ks], preferred_element_type=f32)
                o = part if o is None else o + part
        if nb is not None:
            acc[a2] = acc[a2] * alb[...] + o
        if na is not None:
            m_new = jnp.maximum(m_old, jnp.max(mx, axis=1, keepdims=True))
            m_ref[a] = m_new
            mna[...] = m_new
            ala[...] = jnp.exp2(m_old - m_new)

    def before(n):
        c = lax.div(n, 5)
        i = lax.rem(n, 5)

        @pl.when(jnp.logical_and(i == 2, c < NBLK - 1))
        def _():
            arrive(c + 1)

        @pl.when(jnp.logical_and(i == 0, n < PAIRS))
        def _():
            ready(c)

    def finish(n):
        a, c = pair_of(n)
        i = lax.rem(n, 5)
        last = (jnp.logical_and(i == 4, c == 15))
        for b in range(4):
            last = jnp.logical_or(last, jnp.logical_and(i == b, lax.div(c, 1 << b) == (16 >> b) - 1))

        @pl.when(last)
        def _():
            y = acc[a]
            y = y / y[:, :1]
            y = y.astype(bf16)
            z = jnp.concatenate([y[:ROWS, 64:], y[ROWS:, 64:]], axis=1)
            osend[pl.ds(a * 4, 4)] = z.reshape(4, PART, 128)

            @pl.loop(0, 4)
            def _(w):
                t = a * 4 + w
                to = xor(chip, t, 6)

                @pl.when(t > 0)
                def _():
                    pltpu.make_async_remote_copy(
                        osend.at[t], obuf.at[chip], o_send, o_recv,
                        device_id=dev(to), device_id_type=MESH_ID,
                    ).start()

                @pl.when(t == 0)
                def _():
                    own = pltpu.make_async_copy(osend.at[t], obuf.at[chip], loc.at[2])
                    own.start()
                    own.wait()

    ready(0)
    stage(0, None, s0, s1, al0, al1, mn0, mn1)

    @pl.loop(0, PAIRS // 2)
    def _(h):
        n = h * 2
        before(n + 1)
        stage(n + 1, n, s1, s0, al1, al0, mn1, mn0)
        before(n + 2)
        stage(jnp.minimum(n + 2, PAIRS - 1), n + 1, s0, s1, al0, al1, mn0, mn1)

        @pl.loop(0, 2)
        def _(u):
            finish(n + u)

    def done(ref, sem):
        return pltpu.make_async_remote_copy(
            ref, ref, sem, sem, device_id=sibling, device_id_type=MESH_ID
        )

    done(obuf.at[pl.ds(0, CHIPS - 1)], o_recv).wait_recv()

    @pl.loop(0, HEADS // 2)
    def _(g):
        cols = pl.ds(pl.multiple_of(g * 128, 128), 128)
        for c in range(2):
            e = obuf[g * 4 + c]
            o = obuf[g * 4 + 2 + c]
            out_ref[c * 128:c * 128 + 64, cols] = jnp.concatenate([e[:, :64], o[:, :64]], axis=1)
            out_ref[c * 128 + 64:c * 128 + 128, cols] = jnp.concatenate(
                [e[:, 64:], o[:, 64:]], axis=1
            )

    done(osend.at[pl.ds(0, CHIPS - 1)], o_send).wait_send()
    done(qb.at[pl.ds(0, CHIPS - 1)], q_send).wait_send()
    done(kvb.at[0, pl.ds(0, CHIPS - 1)], kv_send).wait_send()
    done(kvb.at[0], f_send).wait_send()


def on_device(qkv):
    vmem = pltpu.VMEM
    bf16, f32 = jnp.bfloat16, jnp.float32
    dma = pltpu.SemaphoreType.DMA
    return pl.pallas_call(
        kernel,
        name="butterfly",
        out_shape=jax.ShapeDtypeStruct((ROWS, D), bf16),
        in_specs=[pl.BlockSpec(memory_space=vmem)],
        out_specs=pl.BlockSpec(memory_space=vmem),
        scratch_shapes=[
            vmem((CHIPS, PART, 128), bf16),
            vmem((HEADS, ROWS, 128), bf16),
            vmem((CHIPS, PART, 128), bf16),
            vmem((2, CHIPS, ROWS, 128), bf16),
            vmem((NBLK, QT, 128), bf16),
            vmem((2, BLOCK, 128), bf16),
            vmem((2, BLOCK, 128), bf16),
            vmem((NBLK, QT, 128), f32),
            vmem((NBLK, QT, 128), f32),
            vmem((QT, BLOCK), f32),
            vmem((QT, BLOCK), f32),
            vmem((QT, 128), f32),
            vmem((QT, 128), f32),
            vmem((QT, 128), f32),
            vmem((QT, 128), f32),
            vmem((CHIPS, PART, 128), bf16),
            vmem((CHIPS, PART, 128), bf16),
            dma, dma, dma, dma((NBLK,)), dma, dma((NBLK,)), dma, dma, dma((3,)),
        ],
        compiler_params=pltpu.CompilerParams(
            collective_id=0, has_side_effects=True, vmem_limit_bytes=60 * 2**20
        ),
    )(qkv)


def solution(mesh):
    spec = P(("blk", "head"), None)
    return jax.shard_map(
        on_device, mesh=mesh, in_specs=(spec,), out_specs=spec, check_vma=False
    )
```

time: 477 us -> 192 us (0.40)
  Pallas kernels: 0 us -> 187 us
  matrix products: 142 us -> 0 us
  waiting for transfers between devices: 136 us -> 0 us
  other arithmetic: 71.9 us -> 0 us
  local copies, waits for them, and re-layouts: 72.3 us -> 2.3 us
  blocking collectives: 23.8 us -> 0 us
  between operations: 14.4 us -> 0.01 us
  starting transfers between devices: 9.34 us -> 0 us
    pallas_call x0 -> x1, Pallas kernels: none -> 187 us  [on_device(): pl.pallas_call(kernel, name='butterfly', out_shape=jax.ShapeDtypeStruct((...]
    dot_general x80 -> x0, matrix products: 142 us -> none  [the longest x40 87 us: one_tile(): jnp.einsum('hqk,khd->hqd', probs, values, preferred_element_type=jnp.floa...]
    all_gather x1 -> x0, waiting for transfers between devices: 83.3 us -> none  [on_device(): gathered = lax.all_gather(pairs, 'blk', axis=0, tiled=True)]
    reduce_sum x40 -> x0, other arithmetic: 65.6 us -> none  [one_tile(): total = jnp.sum(probs.astype(jnp.float32), axis=-1)]
    all_to_all x1 -> x0, waiting for transfers between devices: 52.6 us -> none  [on_device(): lax.all_to_all(shaped, 'head', split_axis=2, concat_axis=0, tiled=True)]
    all_to_all x1 -> x0, blocking collectives: 23.8 us -> none  [on_device(): lax.all_to_all(outputs, 'head', split_axis=0, concat_axis=1, tiled=True)]
    reshape x2 -> x0, local copies, waits for them, and re-layouts: 21.4 us -> none  [the longest x1 17.2 us: on_device(): shaped = qkv.reshape(rows, 3, heads_cols)]
    slice x4 -> x0, local copies, waits for them, and re-layouts: 13.6 us -> none  [the longest x1 5.24 us: on_device(): partials[j].append(attend(queries[j], chosen))]
  transfers between devices with their start and end apart: 2 -> 0, of which waited for: 2 -> 0; matrix products, arithmetic and copies ran while one was open for 20% -> 0% of each run, Pallas kernels for 0% -> 0%
where the time goes in v1:
time: 192 us; the launch traced here: 189 us
  Pallas kernels  187 us (97%)
  local copies, waits for them, and re-layouts  2.3 us (1%)
    pallas_call x1, Pallas kernels, on_device(): pl.pallas_call(kernel, name='butterfly', out_shape=jax.ShapeDtypeStruct((...  187 us

profile of v1, /device:TPU:1, one launch (start us, length us, event | category | flops | bytes accessed | tf_op | source)
XLA Modules:
  0.0 189.4 jit_solution(14289455290062742396)
XLA Ops:
  0.0 187.1 %butterfly.1 = bf16[256,2048]{1,0:T(8,128)(2,1)} custom-call(bf16[256,6144]{1,0:T(8,128)(2,1)} %x_ref.1), custom_call_target="tpu_custom_call" | custom-call | tf_op jit(solution)/shard_map/butterfly/pallas_call | solution.py:285
  187.1 2.3 %copy.3 = bf16[256,2048]{1,0:T(8,128)(2,1)} copy(bf16[256,2048]{1,0:T(8,128)(2,1)} %butterfly.1) | data formatting | bytes 2097152

commit v2 on v1

v2 whole, which is shorter than its diff:
```python
import math

import jax
import jax.numpy as jnp
from jax import lax
from jax.experimental import pallas as pl
from jax.experimental.pallas import tpu as pltpu
from jax.sharding import PartitionSpec as P

HEAD_DIM = 64
BLOCK = 2048
NBLK = 16
HEADS = 32
D = HEADS * HEAD_DIM
CHIPS = 64
ROWS = 256
PART = 64
QT = 512
KC = 512
PAIRS = 5 * NBLK
SCALE = HEAD_DIM**-0.5 * math.log2(math.e)
MESH_ID = pl.DeviceIdType.MESH


def over_bits(count, body):
    def level(bits):
        if len(bits) == count:
            body(*bits)
            return

        @pl.loop(0, 2)
        def _(b):
            level(bits + (b,))

    level(())


def kernel(
    x_ref, out_ref,
    sendq, sendkv, qb, kvb, qs, va, m_ref, acc, s0, s1, al0, al1, mn0, mn1, osend, obuf,
    q_send, q_recv, kv_send, kv_recv, f_send, f_recv, o_send, o_recv, loc,
):
    blk = lax.axis_index("blk")
    head = lax.axis_index("head")
    chip = blk * 8 + lax.div(head, 2)
    core = lax.rem(head, 2)
    f32, bf16 = jnp.float32, jnp.bfloat16

    flip = []
    for i in range(6):
        w = 32 >> i
        flip.append(w * (1 - 2 * lax.rem(lax.div(chip, w), 2)))
    sibling = (blk, head + 1 - 2 * core)

    def every_chip(body):
        def four(b5, b4, b3, b2):
            r = 8 * b5 + 4 * b4 + 2 * b3 + b2
            high = b5 * flip[0] + b4 * flip[1] + b3 * flip[2]
            to_blk = blk + lax.div(high, 8)
            for w in range(4):
                mid = b2 * flip[3] + (w // 2) * flip[4]
                low = mid + (w % 2) * flip[5]
                to = chip + high + low
                owned = half + lax.div(high + mid, 2)
                device = (to_blk, head + 2 * low)
                if w:
                    body(r * 4 + w, to, owned, device)
                else:

                    @pl.when(r > 0)
                    def _():
                        body(r * 4, to, owned, device)

        over_bits(4, four)

    half = lax.div(chip, 2)
    barrier = pltpu.get_barrier_semaphore()

    @every_chip
    def _(t, to, owned, device):
        pl.semaphore_signal(barrier, inc=1, device_id=device, device_id_type=MESH_ID)

    pl.semaphore_signal(barrier, inc=1, device_id=sibling, device_id_type=MESH_ID)

    @pl.loop(0, HEADS // 2)
    def _(g):
        x = x_ref[:, pl.ds(pl.multiple_of(g * 128, 128), 128)]
        for e in range(2):
            y = x[:, e * 64:(e + 1) * 64]
            for c in range(2):
                sendq[g * 4 + e * 2 + c] = jnp.concatenate(
                    [y[c * 128:c * 128 + 64], y[c * 128 + 64:c * 128 + 128]], axis=1
                )

    @pl.loop(0, HEADS // 2)
    def _(g):
        k = x_ref[:, pl.ds(pl.multiple_of(D + g * 128, 128), 128)]
        v = x_ref[:, pl.ds(pl.multiple_of(2 * D + g * 128, 128), 128)]
        for e in range(2):
            h = slice(e * 64, (e + 1) * 64)
            sendkv[g * 2 + e] = jnp.concatenate([k[:, h], v[:, h]], axis=1)

    pl.semaphore_wait(barrier, CHIPS)

    def place(b3, b2, b1, b0, w):
        high = b3 * flip[0] + b2 * flip[1] + b1 * flip[2]
        mid = b0 * flip[3] + (w // 2) * flip[4]
        low = mid + (w % 2) * flip[5]
        return chip + high + low, half + lax.div(high + mid, 2), (blk + lax.div(high, 8), head + 2 * low)

    def bits_of(r):
        return [lax.div(r, 8 >> i) - 2 * lax.div(r, 16 >> i) for i in range(4)]

    def send_q(r):
        for w in range(4):
            if r == 0 and w == 0:
                continue
            to, _, device = place(*[(r >> (3 - i)) & 1 for i in range(4)], w)
            pltpu.make_async_remote_copy(
                sendq.at[to], qb.at[r * 4 + w], q_send, q_recv.at[r],
                device_id=device, device_id_type=MESH_ID,
            ).start()

    def send_kv(r):
        static = isinstance(r, int)
        bits = [(r >> (3 - i)) & 1 for i in range(4)] if static else bits_of(r)
        for w in range(4):
            if static and r == 0 and w == 0:
                continue
            _, owned, device = place(*bits, w)
            pltpu.make_async_remote_copy(
                sendkv.at[owned], kvb.at[core, r * 4 + w], kv_send, kv_recv.at[r],
                device_id=device, device_id_type=MESH_ID,
            ).start()

    for r in (0, 1, 2, 4, 8):
        send_q(r)
    send_kv(0)
    for r in (3, 5, 9):
        send_q(r)
    send_kv(1)

    own_q = pltpu.make_async_copy(sendq.at[chip], qb.at[0], loc.at[0])
    own_kv = pltpu.make_async_copy(sendkv.at[half], kvb.at[core, 0], loc.at[1])
    own_q.start()
    own_kv.start()

    def forward(c):
        rows = pl.ds(c * 4, 4)
        return pltpu.make_async_remote_copy(
            kvb.at[core, rows], kvb.at[core, rows], f_send, f_recv.at[c],
            device_id=sibling, device_id_type=MESH_ID,
        )

    def landed(c, skip):
        part = kvb.at[core, pl.ds(c * 4 + skip, 4 - skip)]
        pltpu.make_async_remote_copy(
            part, part, kv_send, kv_recv.at[c], device_id=sibling, device_id_type=MESH_ID
        ).wait_recv()

    def arrive(c):
        landed(c, 0)
        forward(c).start()

    def ready(c, slot):
        part = kvb.at[1 - core, pl.ds(c * 4, 4)]
        pltpu.make_async_remote_copy(
            part, part, f_send, f_recv.at[c], device_id=sibling, device_id_type=MESH_ID
        ).wait_recv()
        low = lax.broadcasted_iota(jnp.int32, (ROWS, 128), 1) < 64

        @pl.loop(0, 2)
        def _(z):
            for w in range(4):
                t = kvb[z, c * 4 + w]
                rows = pl.ds(pl.multiple_of((z * 4 + w) * ROWS, ROWS), ROWS)
                va[slot, rows] = jnp.where(low, jnp.ones_like(t), t)

    own_kv.wait()
    landed(0, 1)
    forward(0).start()

    m_ref[...] = jnp.full_like(m_ref, -jnp.inf)
    acc[...] = jnp.zeros_like(acc)

    own_q.wait()
    def queries(a, own=0):
        got = qb.at[pl.ds(a * 4 + own, 4 - own)]
        pltpu.make_async_remote_copy(
            got, got, q_send, q_recv.at[a], device_id=sibling, device_id_type=MESH_ID
        ).wait_recv()
        x = qb[pl.ds(a * 4, 4)].reshape(ROWS, 128)
        zero = jnp.zeros((ROWS, 64), bf16)
        qs[a, 0:ROWS] = jnp.concatenate([x[:, :64], zero], axis=1)
        qs[a, ROWS:QT] = jnp.concatenate([x[:, 64:], zero], axis=1)

    queries(0, 1)

    def stage(na, nb, sa, sb, ala, alb, mna, mnb):
        if na is not None:
            a, c, _ = na
            q = qs[a]
            m_old = m_ref[a]
            mx = None
        if nb is not None:
            a2, _, vslot = nb
            m_b = mnb[...]
            o = None
        for j in range(BLOCK // KC):
            ks = slice(j * KC, (j + 1) * KC)
            if na is not None:
                s = lax.dot_general(
                    q,
                    kvb[j // 2, pl.ds(c * 4 + 2 * (j % 2), 2)].reshape(KC, 128),
                    (((1,), (1,)), ((), ())),
                    preferred_element_type=f32,
                )
                sa[:, ks] = s
                for l in range(KC // 128):
                    t = s[:, l * 128:(l + 1) * 128]
                    mx = t if mx is None else jnp.maximum(mx, t)
            if nb is not None:
                ps = []
                for l in range(KC // 128):
                    at = j * KC + l * 128
                    ps.append(jnp.exp2((sb[:, at:at + 128] - m_b) * SCALE).astype(bf16))
                p = jnp.concatenate(ps, axis=1)
                part = jnp.dot(p, va[vslot, ks], preferred_element_type=f32)
                o = part if o is None else o + part
        if nb is not None:
            acc[a2] = acc[a2] * alb[...] + o
        if na is not None:
            m_new = jnp.maximum(m_old, jnp.max(mx, axis=1, keepdims=True))
            m_ref[a] = m_new
            mna[...] = m_new
            ala[...] = jnp.exp2((m_old - m_new) * SCALE)

    def finish(a, last):
        @pl.when(last)
        def _():
            y = acc[a]
            total = jnp.concatenate([y[:ROWS, :64], y[ROWS:, :64]], axis=1)
            z = jnp.concatenate([y[:ROWS, 64:], y[ROWS:, 64:]], axis=1)
            z = (z / total).astype(bf16)
            osend[pl.ds(a * 4, 4)] = z.reshape(4, PART, 128)
            b3 = lax.div(a, 8)
            b2 = lax.div(a, 4) - 2 * b3
            b1 = lax.div(a, 2) - 4 * b3 - 2 * b2
            b0 = a - 8 * b3 - 4 * b2 - 2 * b1
            high = b3 * flip[0] + b2 * flip[1] + b1 * flip[2]
            for w in range(4):
                low = b0 * flip[3] + (w // 2) * flip[4] + (w % 2) * flip[5]

                def send():
                    pltpu.make_async_remote_copy(
                        osend.at[a * 4 + w], obuf.at[chip], o_send, o_recv,
                        device_id=(blk + lax.div(high, 8), head + 2 * low), device_id_type=MESH_ID,
                    ).start()

                if w:
                    send()
                else:
                    pl.when(a > 0)(send)

                    @pl.when(a == 0)
                    def _():
                        own = pltpu.make_async_copy(osend.at[0], obuf.at[chip], loc.at[2])
                        own.start()
                        own.wait()

    even, odd = (s0, al0, mn0), (s1, al1, mn1)

    def step(na, nb, turn):
        x, y = (odd, even) if turn else (even, odd)
        stage(na, nb, x[0], y[0], x[1], y[1], x[2], y[2])

    ready(0, 0)
    queries(1)
    step((1, 0, 0), None, 0)

    def two_blocks(b3, b2, b1):
        h = 4 * b3 + 2 * b2 + b1
        more = h < NBLK // 2 - 1
        pairs, lasts, news = [], [], []
        for b0 in range(2):
            c = 2 * h + b0
            ones = [b3 * b2 * b1 * b0, b3 * b2 * b1, b3 * b2, b3, b3 * b2 * b1 * b0]
            fresh = [b3 + b2 + b1 == 0, b3 + b2 + b1 == 0, b3 + b2 == 0, b3 == 0]
            near = [1 - 2 * b0, 2 - 4 * b1, 4 - 8 * b2, 8 - 16 * b3, 0]
            for i in range(5):
                pairs.append((c + near[i], c, b0))
                news.append(fresh[i] if i < 4 and not (b0 and i == 0) else None)
                lasts.append(None if i in (0, 4) and b0 == 0 else ones[i] == 1)
        for k in range(10):
            if k in (0, 2, 4, 6):

                @pl.when(h < (4 if k < 4 else 3))
                def _():
                    send_kv(4 * h + 2 + k // 2)

            later_q = {1: (6, 10), 3: (7, 11), 5: (12, 13), 7: (14, 15)}.get(k, ())
            if later_q:

                @pl.when(h == 0)
                def _():
                    for r in later_q:
                        send_q(r)

            if k == 1:
                arrive(2 * h + 1)
            if k == 4:
                ready(2 * h + 1, 1)
            if k == 6:

                @pl.when(more)
                def _():
                    arrive(2 * h + 2)

            turn = (k + 1) % 2
            if k < 9:
                if news[k + 1] is not None:
                    pl.when(news[k + 1])(lambda: queries(pairs[k + 1][0]))
                step(pairs[k + 1], pairs[k], turn)
            else:

                @pl.when(more)
                def _():
                    ready(2 * h + 2, 0)
                    step((2 * h + 3, 2 * h + 2, 0), pairs[9], turn)

                @pl.when(jnp.logical_not(more))
                def _():
                    step(None, pairs[9], turn)

            if lasts[k] is not None:
                finish(pairs[k][0], lasts[k])

    over_bits(3, two_blocks)

    def done(ref, sem):
        return pltpu.make_async_remote_copy(
            ref, ref, sem, sem, device_id=sibling, device_id_type=MESH_ID
        )

    done(obuf.at[pl.ds(0, CHIPS - 1)], o_recv).wait_recv()

    @pl.loop(0, HEADS // 2)
    def _(g):
        cols = pl.ds(pl.multiple_of(g * 128, 128), 128)
        for c in range(2):
            e = obuf[g * 4 + c]
            o = obuf[g * 4 + 2 + c]
            out_ref[c * 128:c * 128 + 64, cols] = jnp.concatenate([e[:, :64], o[:, :64]], axis=1)
            out_ref[c * 128 + 64:c * 128 + 128, cols] = jnp.concatenate(
                [e[:, 64:], o[:, 64:]], axis=1
            )

    done(osend.at[pl.ds(0, CHIPS - 1)], o_send).wait_send()
    done(qb.at[pl.ds(0, CHIPS - 1)], q_send).wait_send()
    done(kvb.at[0, pl.ds(0, CHIPS - 1)], kv_send).wait_send()
    done(kvb.at[0], f_send).wait_send()


def on_device(qkv):
    vmem = pltpu.VMEM
    bf16, f32 = jnp.bfloat16, jnp.float32
    dma = pltpu.SemaphoreType.DMA
    return pl.pallas_call(
        kernel,
        name="butterfly",
        out_shape=jax.ShapeDtypeStruct((ROWS, D), bf16),
        in_specs=[pl.BlockSpec(memory_space=vmem)],
        out_specs=pl.BlockSpec(memory_space=vmem),
        scratch_shapes=[
            vmem((CHIPS, PART, 128), bf16),
            vmem((HEADS, ROWS, 128), bf16),
            vmem((CHIPS, PART, 128), bf16),
            vmem((2, CHIPS, ROWS, 128), bf16),
            vmem((NBLK, QT, 128), bf16),
            vmem((2, BLOCK, 128), bf16),
            vmem((NBLK, QT, 128), f32),
            vmem((NBLK, QT, 128), f32),
            vmem((QT, BLOCK), f32),
            vmem((QT, BLOCK), f32),
            vmem((QT, 128), f32),
            vmem((QT, 128), f32),
            vmem((QT, 128), f32),
            vmem((QT, 128), f32),
            vmem((CHIPS, PART, 128), bf16),
            vmem((CHIPS, PART, 128), bf16),
            dma, dma((NBLK,)), dma, dma((NBLK,)), dma, dma((NBLK,)), dma, dma, dma((3,)),
        ],
        compiler_params=pltpu.CompilerParams(
            collective_id=0, has_side_effects=True, vmem_limit_bytes=60 * 2**20
        ),
    )(qkv)


def solution(mesh):
    spec = P(("blk", "head"), None)
    return jax.shard_map(
        on_device, mesh=mesh, in_specs=(spec,), out_specs=spec, check_vma=False
    )
```

time: 192 us -> 160 us (0.83); the launches traced: 189 us -> 159 us
  Pallas kernels: 187 us -> 157 us
    pallas_call x1, Pallas kernels: 187 us -> 157 us  [on_device(): pl.pallas_call(kernel, name='butterfly', out_shape=jax.ShapeDtypeStruct((...]
where the time goes in v2:
time: 160 us; the launch traced here: 159 us
  Pallas kernels  157 us (98%)
  local copies, waits for them, and re-layouts  2.3 us (1%)
    pallas_call x1, Pallas kernels, on_device(): pl.pallas_call(kernel, name='butterfly', out_shape=jax.ShapeDtypeStruct((...  157 us

profile of v2, /device:TPU:1, one launch (start us, length us, event | category | flops | bytes accessed | tf_op | source)
XLA Modules:
  0.0 159.3 jit_solution(4135626008247623732)
XLA Ops:
  0.0 157.0 %butterfly.1 = bf16[256,2048]{1,0:T(8,128)(2,1)} custom-call(bf16[256,6144]{1,0:T(8,128)(2,1)} %x_ref.1), custom_call_target="tpu_custom_call" | custom-call | tf_op jit(solution)/shard_map/butterfly/pallas_call | solution.py:368
  157.0 2.3 %copy.3 = bf16[256,2048]{1,0:T(8,128)(2,1)} copy(bf16[256,2048]{1,0:T(8,128)(2,1)} %butterfly.1) | data formatting | bytes 2097152

commit v3 on v2

--- a/solution.py
+++ b/solution.py
@@ -36,8 +36,8 @@
 
 
 def kernel(
-    x_ref, out_ref,
-    sendq, sendkv, qb, kvb, qs, va, m_ref, acc, s0, s1, al0, al1, mn0, mn1, osend, obuf,
+    qkv_ref, out_ref,
+    x_ref, sendq, sendkv, qb, kvb, qs, va, m_ref, acc, s0, s1, al0, al1, mn0, mn1, osend, obuf,
     q_send, q_recv, kv_send, kv_recv, f_send, f_recv, o_send, o_recv, loc,
 ):
     blk = lax.axis_index("blk")
@@ -52,35 +52,26 @@
         flip.append(w * (1 - 2 * lax.rem(lax.div(chip, w), 2)))
     sibling = (blk, head + 1 - 2 * core)
 
-    def every_chip(body):
-        def four(b5, b4, b3, b2):
-            r = 8 * b5 + 4 * b4 + 2 * b3 + b2
-            high = b5 * flip[0] + b4 * flip[1] + b3 * flip[2]
-            to_blk = blk + lax.div(high, 8)
-            for w in range(4):
-                mid = b2 * flip[3] + (w // 2) * flip[4]
-                low = mid + (w % 2) * flip[5]
-                to = chip + high + low
-                owned = half + lax.div(high + mid, 2)
-                device = (to_blk, head + 2 * low)
-                if w:
-                    body(r * 4 + w, to, owned, device)
-                else:
-
-                    @pl.when(r > 0)
-                    def _():
-                        body(r * 4, to, owned, device)
-
-        over_bits(4, four)
-
     half = lax.div(chip, 2)
+    def place(b3, b2, b1, b0, w):
+        high = b3 * flip[0] + b2 * flip[1] + b1 * flip[2]
+        mid = b0 * flip[3] + (w // 2) * flip[4]
+        low = mid + (w % 2) * flip[5]
+        return chip + high + low, half + lax.div(high + mid, 2), (blk + lax.div(high, 8), head + 2 * low)
+
+    load = pltpu.make_async_copy(qkv_ref, x_ref, loc.at[3])
+    load.start()
     barrier = pltpu.get_barrier_semaphore()
 
-    @every_chip
-    def _(t, to, owned, device):
-        pl.semaphore_signal(barrier, inc=1, device_id=device, device_id_type=MESH_ID)
+    for r in range(NBLK):
+        for w in range(4):
+            if r + w:
+                _, _, device = place(*[(r >> (3 - i)) & 1 for i in range(4)], w)
+                pl.semaphore_signal(barrier, inc=1, device_id=device, device_id_type=MESH_ID)
 
     pl.semaphore_signal(barrier, inc=1, device_id=sibling, device_id_type=MESH_ID)
+
+    load.wait()
 
     @pl.loop(0, HEADS // 2)
     def _(g):
@@ -101,12 +92,6 @@
             sendkv[g * 2 + e] = jnp.concatenate([k[:, h], v[:, h]], axis=1)
 
     pl.semaphore_wait(barrier, CHIPS)
-
-    def place(b3, b2, b1, b0, w):
-        high = b3 * flip[0] + b2 * flip[1] + b1 * flip[2]
-        mid = b0 * flip[3] + (w // 2) * flip[4]
-        low = mid + (w % 2) * flip[5]
-        return chip + high + low, half + lax.div(high + mid, 2), (blk + lax.div(high, 8), head + 2 * low)
 
     def bits_of(r):
         return [lax.div(r, 8 >> i) - 2 * lax.div(r, 16 >> i) for i in range(4)]
@@ -133,9 +118,9 @@
                 device_id=device, device_id_type=MESH_ID,
             ).start()
 
-    for r in (0, 1, 2, 4, 8):
+    send_kv(0)
+    for r in (1, 2, 4, 8, 0):
         send_q(r)
-    send_kv(0)
     for r in (3, 5, 9):
         send_q(r)
     send_kv(1)
@@ -369,9 +354,10 @@
         kernel,
         name="butterfly",
         out_shape=jax.ShapeDtypeStruct((ROWS, D), bf16),
-        in_specs=[pl.BlockSpec(memory_space=vmem)],
+        in_specs=[pl.BlockSpec(memory_space=pl.ANY)],
         out_specs=pl.BlockSpec(memory_space=vmem),
         scratch_shapes=[
+            vmem((ROWS, 3 * D), bf16),
             vmem((CHIPS, PART, 128), bf16),
             vmem((HEADS, ROWS, 128), bf16),
             vmem((CHIPS, PART, 128), bf16),
@@ -388,7 +374,7 @@
             vmem((QT, 128), f32),
             vmem((CHIPS, PART, 128), bf16),
             vmem((CHIPS, PART, 128), bf16),
-            dma, dma((NBLK,)), dma, dma((NBLK,)), dma, dma((NBLK,)), dma, dma, dma((3,)),
+            dma, dma((NBLK,)), dma, dma((NBLK,)), dma, dma((NBLK,)), dma, dma, dma((4,)),
         ],
         compiler_params=pltpu.CompilerParams(
             collective_id=0, has_side_effects=True, vmem_limit_bytes=60 * 2**20

time: 160 us -> 168 us (1.050); the launches traced: 159 us -> 165 us
  Pallas kernels: 157 us -> 163 us
    pallas_call x1, Pallas kernels: 157 us -> 163 us  [on_device(): pl.pallas_call(kernel, name='butterfly', out_shape=jax.ShapeDtypeStruct((...]
where the time goes in v3:
time: 168 us; the launch traced here: 165 us
  Pallas kernels  163 us (97%)
  local copies, waits for them, and re-layouts  2.3 us (1%)
    pallas_call x1, Pallas kernels, on_device(): pl.pallas_call(kernel, name='butterfly', out_shape=jax.ShapeDtypeStruct((...  163 us

profile of v3, /device:TPU:1, one launch (start us, length us, event | category | flops | bytes accessed | tf_op | source)
XLA Modules:
  0.0 165.4 jit_solution(12321446351022583807)
XLA Ops:
  0.0 163.1 %butterfly.1 = bf16[256,2048]{1,0:T(8,128)(2,1)} custom-call(bf16[256,6144]{1,0:T(8,128)(2,1)} %qkv_ref.1), custom_call_target="tpu_custom_call" | custom-call | tf_op jit(solution)/shard_map/butterfly/pallas_call | solution.py:353
  163.1 2.3 %copy.3 = bf16[256,2048]{1,0:T(8,128)(2,1)} copy(bf16[256,2048]{1,0:T(8,128)(2,1)} %butterfly.1) | data formatting | bytes 2097152

commit v4 on v2

--- a/solution.py
+++ b/solution.py
@@ -112,10 +112,12 @@
         return [lax.div(r, 8 >> i) - 2 * lax.div(r, 16 >> i) for i in range(4)]
 
     def send_q(r):
+        static = isinstance(r, int)
+        bits = [(r >> (3 - i)) & 1 for i in range(4)] if static else bits_of(r)
         for w in range(4):
-            if r == 0 and w == 0:
+            if static and r == 0 and w == 0:
                 continue
-            to, _, device = place(*[(r >> (3 - i)) & 1 for i in range(4)], w)
+            to, _, device = place(*bits, w)
             pltpu.make_async_remote_copy(
                 sendq.at[to], qb.at[r * 4 + w], q_send, q_recv.at[r],
                 device_id=device, device_id_type=MESH_ID,
@@ -133,11 +135,19 @@
                 device_id=device, device_id_type=MESH_ID,
             ).start()
 
-    for r in (0, 1, 2, 4, 8):
-        send_q(r)
+    send_q(0)
+
+    @pl.loop(0, 4)
+    def _(u):
+        square = lax.div(u * (u - 1), 2)
+        send_q(1 + u + square + lax.div(square * (u - 2), 3))
+
     send_kv(0)
-    for r in (3, 5, 9):
-        send_q(r)
+
+    @pl.loop(0, 3)
+    def _(u):
+        send_q(3 + 2 * u + u * (u - 1))
+
     send_kv(1)
 
     own_q = pltpu.make_async_copy(sendq.at[chip], qb.at[0], loc.at[0])
@@ -298,13 +308,14 @@
                 def _():
                     send_kv(4 * h + 2 + k // 2)
 
-            later_q = {1: (6, 10), 3: (7, 11), 5: (12, 13), 7: (14, 15)}.get(k, ())
+            later_q = {1: (6, 4), 3: (7, 4), 5: (12, 1), 7: (14, 1)}.get(k)
             if later_q:
 
                 @pl.when(h == 0)
                 def _():
-                    for r in later_q:
-                        send_q(r)
+                    @pl.loop(0, 2)
+                    def _(u):
+                        send_q(later_q[0] + later_q[1] * u)
 
             if k == 1:
                 arrive(2 * h + 1)

time: 160 us -> 160 us (level)
  no operation moved by 1% of the time
where the time goes in v4:
time: 160 us; the launch traced here: 159 us
  Pallas kernels  157 us (98%)
  local copies, waits for them, and re-layouts  2.3 us (1%)
    pallas_call x1, Pallas kernels, on_device(): pl.pallas_call(kernel, name='butterfly', out_shape=jax.ShapeDtypeStruct((...  157 us

profile of v4, /device:TPU:1, one launch (start us, length us, event | category | flops | bytes accessed | tf_op | source)
XLA Modules:
  0.0 159.3 jit_solution(10025269421653322958)
XLA Ops:
  0.0 157.0 %butterfly.1 = bf16[256,2048]{1,0:T(8,128)(2,1)} custom-call(bf16[256,6144]{1,0:T(8,128)(2,1)} %x_ref.1), custom_call_target="tpu_custom_call" | custom-call | tf_op jit(solution)/shard_map/butterfly/pallas_call | solution.py:379
  157.0 2.3 %copy.3 = bf16[256,2048]{1,0:T(8,128)(2,1)} copy(bf16[256,2048]{1,0:T(8,128)(2,1)} %butterfly.1) | data formatting | bytes 2097152
